TPU v7x, 512 devices: a whole 4x4x16 slice. The times are simulated.
512 devices in a mesh: row: 64 (over x, z), col: 8 (over y, core).
Axes of the slice: x: 4, y: 4, z: 16, core: 2. Of those that a mesh axis runs over, the one named last changes fastest.
Arguments:
- inverse_kernel: float32 [8192, 8192], P('row', 'col'), as said below
- points: bfloat16 [8192, 1024], P('row', 'col')
- candidates: bfloat16 [1024, 1024], P(None, 'col')
- obs_embed: float32 [8192], P('row'), may hold values from 0.5 to 5
- cand_embed: float32 [1024], replicated, may hold values from 0.05 to 0.5
- chosen: int32 [64], replicated, may hold values from 0 to 1023, as said below
Outputs:
- inverse_update: float32 [8192, 8192], P('row', 'col')
- schur_inverse: float32 [64, 64], replicated
- new_weights: float32 [64], replicated
- weight_shift: float32 [8192], P('row')
Inputs may be any that keep to these rules, and one draw needn't show every extreme that they name: inverse_kernel is symmetric. `chosen`: the indices are distinct.
All inputs are finite; a program needn't handle non-finite values.
Results may differ from a plain program's by a relative error of at most 0.0003.
Values sent between devices are 32-bit elements; how exact they have to be, the bound alone decides.
A program may use at most 64 MiB of HBM per device.

v0:
```python
import jax
import jax.numpy as jnp
from jax import lax
from jax.sharding import PartitionSpec as P


def matern(square):
    scaled = jnp.sqrt(5.0 * jnp.maximum(square, 0.0))
    return (1.0 + scaled + scaled * scaled / 3.0) * jnp.exp(-scaled)


def on_device(inverse_kernel, points, candidates, obs_embed, cand_embed, chosen):
    high = lax.Precision.HIGHEST
    rows = inverse_kernel.shape[0]
    cols = inverse_kernel.shape[1]
    count_new = chosen.shape[0]
    count_row = lax.axis_size("row")
    nobs = rows * count_row
    onehot = chosen[:, None] == jnp.arange(candidates.shape[0], dtype=jnp.int32)[None, :]
    appended = jnp.dot(
        onehot.astype(jnp.bfloat16), candidates, preferred_element_type=jnp.float32
    ).astype(jnp.bfloat16)
    new_embed = jnp.dot(onehot.astype(jnp.float32), cand_embed, precision=high)
    cross = lax.dot_general(
        points, appended, (((1,), (1,)), ((), ())), preferred_element_type=jnp.float32
    )
    wide = points.astype(jnp.float32)
    sq_obs = jnp.sum(wide * wide, axis=1)
    pair = lax.dot_general(
        appended, appended, (((1,), (1,)), ((), ())), preferred_element_type=jnp.float32
    )
    cross, sq_obs, pair = lax.psum((cross, sq_obs, pair), "col")
    sq_new = jnp.diagonal(pair)
    kvec = matern(sq_obs[:, None] + sq_new[None, :] - 2.0 * cross) * (1.0 / (18.0 * nobs))
    gram = matern(sq_new[:, None] + sq_new[None, :] - 2.0 * pair)
    col_index = lax.axis_index("col")
    kernel_all = lax.all_gather(kvec, "row", axis=0, tiled=True)
    kernel_cols = lax.dynamic_slice_in_dim(kernel_all, col_index * cols, cols, 0)
    partial_rows = jnp.dot(inverse_kernel, kernel_cols, precision=high)
    solved_rows = lax.psum(partial_rows, "col")
    solved_all = lax.all_gather(solved_rows, "row", axis=0, tiled=True)
    solved_cols = lax.dynamic_slice_in_dim(solved_all, col_index * cols, cols, 0)
    kernel_term = lax.dot_general(kvec, solved_rows, (((0,), (0,)), ((), ())), precision=high)
    embed_term = jnp.dot(obs_embed, solved_rows, precision=high)
    kernel_term, embed_term = lax.psum((kernel_term, embed_term), "row")
    identity = jnp.eye(count_new, dtype=jnp.float32)
    schur = identity + gram / count_new - kernel_term
    quad = embed_term / nobs - new_embed
    factor = jnp.linalg.cholesky(schur)
    schur_inverse = jax.scipy.linalg.cho_solve((factor, True), identity)
    new_weights = jnp.dot(schur_inverse, quad, precision=high)
    weight_shift = jnp.dot(solved_rows, new_weights, precision=high)
    left = jnp.dot(solved_rows, schur_inverse, precision=high)
    inverse_update = lax.dot_general(left, solved_cols, (((1,), (1,)), ((), ())), precision=high)
    return (inverse_update, schur_inverse, new_weights, weight_shift)


def solution(mesh):
    return jax.shard_map(
        on_device,
        mesh=mesh,
        in_specs=(P("row", "col"), P("row", "col"), P(None, "col"), P("row"), P(), P()),
        out_specs=(P("row", "col"), P(), P(), P("row")),
        check_vma=False,
    )
```

profile of v0, /device:TPU:8, one launch (start us, length us, event | category | flops | bytes accessed | tf_op | source)
XLA Modules:
  0.0 504.0 jit_solution(14065995295820615962)
XLA Ops:
  7.3 0.9 multiply_reduce_fusion
  8.2 1.2 convolution_convert_fusion
  9.4 0.9 convolution_bitcast_fusion.1
  10.3 0.1 fusion.17
  10.4 26.6 %all-reduce.1 = (f32[128,64]{0,1:T(8,128)S(1)}, f32[64,64]{1,0:T(8,128)S(1)}, f32[128]{0:T(128)S(1)}) all-reduce(f32[128,64]{0,1:T(8,128)S(1)} %convolution_bitcast_fusion.1, f32[64,64]{1,0:T(8,128)S(1)} %fusion.17, f32[128]{0:T(128)S(1)} %multiply_reduce_fusion), channel_id=1, replica_groups=mesh['row'=64,'col'=8] {'col'}, use_global_device_ids=true, to_apply=%region_3.0 | all-reduce | flops 12416 | bytes 99328 | tf_op jit(solution)/shard_map/psum | solution.py:32
  37.0 0.8 gather_fusion
  37.8 0.7 multiply_multiply_fusion
  38.6 137.5 %all-gather.3.cloned.1.call-done = f32[8192,64]{0,1:T(8,128)} async-done(((f32[128,64]{0,1:T(8,128)}), f32[8192,64]{0,1:T(8,128)}) %all-gather.3.cloned.1.call-update) | async-done | bytes 2097168 | tf_op jit(solution)/shard_map/all_gather | solution.py:37
  176.2 1.6 convolution_bitcast_fusion
  177.8 21.3 %psum.45 = f32[128,64]{0,1:T(8,128)} all-reduce(f32[128,64]{0,1:T(8,128)S(1)} %convolution_bitcast_fusion), channel_id=1, replica_groups=mesh['row'=64,'col'=8] {'col'}, use_global_device_ids=true, to_apply=%region_4.5 | all-reduce | flops 8192 | bytes 65536 | tf_op jit(solution)/shard_map/psum | solution.py:40
  199.1 0.9 convolution_bitcast_fusion.3
  200.0 1.0 fusion.18
  201.0 278.2 %all-reduce = (f32[64,64]{1,0:T(8,128)S(1)}, f32[64]{0:T(128)S(1)}) all-reduce(f32[64,64]{1,0:T(8,128)S(1)} %fusion.18, f32[64]{0:T(128)S(1)} %convolution_bitcast_fusion.3), channel_id=1, replica_groups=mesh['row'=64,'col'=8] {'row'}, use_global_device_ids=true, to_apply=%region_5.6 | all-reduce | flops 4160 | bytes 33280 | tf_op jit(solution)/shard_map/psum | solution.py:45
  479.4 5.8 %cholesky.17 = f32[64,64]{1,0:T(8,128)S(1)} custom-call(f32[64,64]{1,0:T(8,128)S(1)} %fusion.12), custom_call_target="Cholesky" | custom-call | tf_op jit(solution)/shard_map/jit(cholesky)/cholesky | solution.py:49
  485.3 0.6 compare_reduce_fusion
  485.9 0.7 fusion.7
  486.6 4.9 custom-call.10
  491.5 0.2 fusion.1
  491.7 0.3 fusion.10
  492.0 0.2 fusion.8
  492.2 0.1 fusion.20
  492.3 1.4 convolution_bitcast_fusion.2
  493.8 1.0 fusion.19
  494.9 2.3 fusion.2
  (22 shorter events, 0.4 us)
Async XLA Ops:
  7.2 169.0 %copy-start = (f32[128,1024]{1,0:T(8,128)S(1)}, f32[128,1024]{1,0:T(8,128)}, u32[]{:S(2)}) copy-start(f32[128,1024]{1,0:T(8,128)} %param.6) | copy-start | bytes 1572868
  7.2 484.3 %copy-start.5 = (s32[64]{0:T(128)S(1)}, s32[64]{0:T(128)}, u32[]{:S(2)}) copy-start(s32[64]{0:T(128)} %param.11) | copy-start | bytes 772
  7.2 191.9 %copy-start.3 = (f32[128]{0:T(128)S(1)}, f32[128]{0:T(128)}, u32[]{:S(2)}) copy-start(f32[128]{0:T(128)} %param.9) | copy-start | bytes 1540
  7.2 484.3 %copy-start.4 = (f32[1024]{0:T(1024)S(1)}, f32[1024]{0:T(1024)}, u32[]{:S(2)}) copy-start(f32[1024]{0:T(1024)} %param.10) | copy-start | bytes 12292
  7.2 169.0 %all-gather.3.cloned.1.call-start = ((), (), s32[]{:S(2)}) async-start(), calls=%async_computation | async-start | bytes 2129920 | tf_op jit(solution)/shard_map/all_gather | solution.py:37
  38.6 456.3 %all-gather.5.cloned.1.call-start = ((), (), s32[]{:S(2)}) async-start(), calls=%async_computation.1 | async-start | bytes 2129920 | tf_op jit(solution)/shard_map/all_gather | solution.py:41
  492.2 5.0 copy-start.1
  492.3 4.8 copy-start.2
Sparse Core Ops, SparseCore 0:
  38.7 137.4 all-gather.2
  199.2 131.8 all-gather.4
where the time goes:
time: 505 us; the launch traced here: 504 us
  blocking collectives  326 us (65%)
  waiting for transfers between devices  138 us (27%)
  between operations  14.2 us (3%)
  other arithmetic  13.8 us (3%)
  matrix products  11.3 us (2%)
    psum x1, blocking collectives, on_device(): kernel_term, embed_term = lax.psum((kernel_term, embed_term), 'row')  278 us
    all_gather x1, waiting for transfers between devices, on_device(): kernel_all = lax.all_gather(kvec, 'row', axis=0, tiled=True)  138 us
    psum x1, blocking collectives, on_device(): cross, sq_obs, pair = lax.psum((cross, sq_obs, pair), 'col')  26.6 us
    psum x1, blocking collectives, on_device(): solved_rows = lax.psum(partial_rows, 'col')  21.3 us
  transfers between devices with their start and end apart: 2, of which 1 were waited for; matrix products, arithmetic and copies ran while one was open for 3% of the time, Pallas kernels for 0%

commit v1 on v0

v1 whole, which is shorter than its diff:
```python
import jax
import jax.numpy as jnp
from jax import lax
from jax.experimental import pallas as pl
from jax.experimental.pallas import tpu as pltpu
from jax.sharding import PartitionSpec as P

MESH = pl.DeviceIdType.MESH
HIGH = lax.Precision.HIGHEST
NX, NY, NZ, NC = 4, 4, 16, 2
NOBS = 8192
NEW = 64


def matern(square):
    scaled = jnp.sqrt(5.0 * jnp.maximum(square, 0.0))
    return (1.0 + scaled + scaled * scaled / 3.0) * jnp.exp(-scaled)


def dot_t(a, b, precision=None):
    return lax.dot_general(
        a, b, (((1,), (1,)), ((), ())), precision=precision, preferred_element_type=jnp.float32
    )


def exchange_kernel(
    inv_hbm, points_ref, cand_ref, embed_ref, chosen_ref,
    total_ref, solved_cols_ref, solved_rows_ref,
    inv, a2a_src, a2a_rcv, tile, full, gsrc, grcv, etr, ebuf, srow, fsrc, frcv,
    ss_a, rs_a, ss_z, rs_z, ss_x, rs_x, ss_g, rs_g, ss_r, rs_r, ss_f, rs_f, ss_e, rs_e, ss_ez, rs_ez, inv_sem,
):
    row = lax.axis_index("row")
    col = lax.axis_index("col")
    x, z = row // NZ, row % NZ
    y, core = col // NC, col % NC
    half = z // 8
    spot = z % 8
    mine = 2 * x + core
    on_diag = x == y
    home = core == half

    def send(src, dst, ssem, rsem, to_row, to_col, is_self):
        remote = pltpu.make_async_remote_copy(
            src_ref=src, dst_ref=dst, send_sem=ssem, recv_sem=rsem,
            device_id=(to_row, to_col), device_id_type=MESH,
        )

        @pl.when(is_self)
        def _():
            pltpu.make_async_copy(src, dst, rsem).start()

        @pl.when(jnp.logical_not(is_self))
        def _():
            remote.start()

    def wait_sent(src, dst, ssem, rsem, to_row, to_col, is_self):
        @pl.when(jnp.logical_not(is_self))
        def _():
            pltpu.make_async_remote_copy(
                src_ref=src, dst_ref=dst, send_sem=ssem, recv_sem=rsem,
                device_id=(to_row, to_col), device_id_type=MESH,
            ).wait_send()

    def arrived(dst, rsem):
        pltpu.make_async_copy(dst, dst, rsem).wait()

    inv_copy = pltpu.make_async_copy(inv_hbm, inv, inv_sem)
    inv_copy.start()

    barrier = pltpu.get_barrier_semaphore()

    def greet(to_row, to_col, is_self):
        @pl.when(jnp.logical_not(is_self))
        def _():
            pl.semaphore_signal(barrier, inc=1, device_id=(to_row, to_col), device_id_type=MESH)

    for k in range(8):
        greet(y * NZ + z, jnp.int32(k), jnp.logical_and(on_diag, col == k))
        greet((k // 2) * NZ + z, x * NC + k % 2, jnp.logical_and(on_diag, mine == k))
        greet(row, jnp.int32(k), col == k)
    for k in range(16):
        greet(x * NZ + core * 8 + k // 2, y * NC + k % 2, jnp.logical_and(row % NZ == core * 8 + k // 2, core == k % 2))
    for k in range(4):
        greet(k * NZ + z, col, x == k)

    onehot = (chosen_ref[...] == lax.broadcasted_iota(jnp.int32, (NEW, cand_ref.shape[0]), 1))
    onehot = jnp.where(onehot, 1.0, 0.0).astype(jnp.bfloat16)
    appended = jnp.dot(onehot, cand_ref[...], preferred_element_type=jnp.float32).astype(jnp.bfloat16)
    pts = points_ref[...]
    wide = pts.astype(jnp.float32)
    sq_obs = dot_t(jnp.ones((8, wide.shape[1]), jnp.float32), wide * wide, HIGH)[0:1]
    pair = dot_t(appended, appended)
    eye = lax.broadcasted_iota(jnp.int32, (NEW, NEW), 0) == lax.broadcasted_iota(jnp.int32, (NEW, NEW), 1)
    diagonal = jnp.where(eye, pair, 0.0)
    sq_col = jnp.sum(diagonal, axis=1, keepdims=True)
    sq_row = jnp.sum(diagonal, axis=0, keepdims=True)
    a2a_src[0] = sq_obs + sq_col - 2.0 * dot_t(appended, pts)
    gsrc[:, 0:NEW] = sq_row + sq_col - 2.0 * pair
    gsrc[:, NEW:] = jnp.zeros((NEW, NEW), jnp.float32)

    pl.semaphore_wait(barrier, 41 - 2 * on_diag.astype(jnp.int32) - home.astype(jnp.int32) + 1)

    def a2a_args(p, e):
        return (
            a2a_src.at[p, pl.ds(8 * e, 8)], a2a_rcv.at[p, col], ss_a.at[p, e], rs_a.at[p, col],
            (e // 2) * NZ + z, x * NC + e % 2, jnp.logical_and(on_diag, mine == e),
        )

    def g_args(k):
        return (gsrc.at[pl.ds(8 * k, 8)], grcv.at[col], ss_g.at[k], rs_g.at[col], row, jnp.int32(k), col == k)

    def z_args(p, k):
        return (
            tile.at[p], full.at[p, x, core, spot], ss_z.at[p, k], rs_z.at[p, core, spot],
            x * NZ + k, y * NC + half, jnp.logical_and(home, z == k),
        )

    def x_args(p, k):
        return (full.at[p, x], full.at[p, x], ss_x.at[p, k], rs_x.at[p, x], k * NZ + z, col)

    def e_args():
        return (embed_ref, etr, ss_e, rs_e, y * NZ + z, x * NC + core, on_diag)

    def ez_args(k):
        return (etr, ebuf.at[spot], ss_ez.at[k], rs_ez.at[spot], x * NZ + k, y * NC + half, z == k)

    def r_args(k):
        return (
            tile.at[1], srow.at[mine], ss_r.at[k], rs_r.at[mine],
            y * NZ + z, jnp.int32(k), jnp.logical_and(on_diag, col == k),
        )

    def f_args(k):
        return (fsrc, frcv.at[col], ss_f.at[k], rs_f.at[col], row, jnp.int32(k), col == k)

    def reduce_tiles(p):
        for e in range(8):
            send(*a2a_args(p, e))

    def reduced(p):
        for k in range(8):
            arrived(a2a_rcv.at[p, k], rs_a.at[p, k])
        value = a2a_rcv[p, 0]
        for k in range(1, 8):
            value = value + a2a_rcv[p, k]
        return value

    def spread_z(p):
        for k in range(NZ):
            send(*z_args(p, k))

    def spread_x(p):
        for c in range(NC):
            for s in range(8):
                arrived(full.at[p, x, c, s], rs_z.at[p, c, s])
        for k in range(NX):
            src, dst, ssem, rsem, to_row, to_col = x_args(p, k)

            @pl.when(x != k)
            def _():
                pltpu.make_async_remote_copy(
                    src_ref=src, dst_ref=dst, send_sem=ssem, recv_sem=rsem,
                    device_id=(to_row, to_col), device_id_type=MESH,
                ).start()

    def spread_done(p):
        for k in range(NX):
            @pl.when(x != k)
            def _():
                arrived(full.at[p, k], rs_x.at[p, k])
        parts = [full[p, :, :, s].reshape(NEW, 128) for s in range(8)]
        return jnp.concatenate(parts, axis=1)

    reduce_tiles(0)
    send(*e_args())
    for k in range(8):
        send(*g_args(k))

    tile[0] = matern(reduced(0)) * (1.0 / (18.0 * NOBS))
    spread_z(0)

    arrived(etr, rs_e)

    @pl.when(home)
    def _():
        for k in range(NZ):
            send(*ez_args(k))

    for k in range(8):
        arrived(grcv.at[k], rs_g.at[k])
    gram = grcv[0]
    for k in range(1, 8):
        gram = gram + grcv[k]
    gram = matern(gram[:, 0:NEW]) * (1.0 / NEW)

    spread_x(0)
    kernel_cols = spread_done(0)
    inv_copy.wait()
    a2a_src[1] = dot_t(kernel_cols, inv[...], HIGH)
    reduce_tiles(1)
    tile[1] = reduced(1)
    spread_z(1)
    for k in range(8):
        send(*r_args(k))
    spread_x(1)
    solved_cols = spread_done(1)
    for s in range(8):
        arrived(ebuf.at[s], rs_ez.at[s])
    embed = jnp.concatenate([ebuf[s] for s in range(8)], axis=1)
    fsrc[:, 0:NEW] = -dot_t(solved_cols, kernel_cols, HIGH)
    fsrc[:, NEW:] = jnp.broadcast_to(jnp.sum(solved_cols * embed, axis=1, keepdims=True), (NEW, NEW))
    slot = pl.ds(pl.multiple_of(8 * col, 8), 8)
    fsrc[slot, 0:NEW] = fsrc[slot, 0:NEW] + gram
    for k in range(8):
        send(*f_args(k))
    solved_cols_ref[...] = solved_cols
    for k in range(8):
        arrived(srow.at[k], rs_r.at[k])
    solved_rows_ref[...] = srow[...].reshape(NEW, 128)
    for k in range(8):
        arrived(frcv.at[k], rs_f.at[k])
    total = frcv[0]
    for k in range(1, 8):
        total = total + frcv[k]
    total_ref[...] = total

    wait_sent(*e_args())
    for p in range(2):
        for k in range(8):
            wait_sent(*a2a_args(p, k))
        for k in range(NZ):
            wait_sent(*z_args(p, k))
        for k in range(NX):
            wait_sent(*x_args(p, k), x == k)
    for k in range(8):
        wait_sent(*g_args(k))
        wait_sent(*r_args(k))
        wait_sent(*f_args(k))

    @pl.when(home)
    def _():
        for k in range(NZ):
            wait_sent(*ez_args(k))


def finish_kernel(
    total_ref, solved_cols_ref, solved_rows_ref, chosen_ref, cand_embed_ref,
    update_ref, inverse_ref, weights_ref, shift_ref,
):
    total = total_ref[...]
    sub = lax.broadcasted_iota(jnp.int32, (NEW, NEW), 0)
    lane = lax.broadcasted_iota(jnp.int32, (NEW, NEW), 1)
    matrix = total[:, 0:NEW] + jnp.where(sub == lane, 1.0, 0.0)
    picked = chosen_ref[...] == lax.broadcasted_iota(jnp.int32, (NEW, cand_embed_ref.shape[1]), 1)
    new_embed = jnp.sum(jnp.where(picked, cand_embed_ref[...], 0.0), axis=1, keepdims=True)
    quad = total[:, NEW:NEW + 1] * (1.0 / NOBS) - new_embed
    for k in range(NEW):
        pivot = matrix[k:k + 1, k:k + 1]
        scale = jnp.where(pivot > 0.0, 1.0 / pivot, jnp.nan)
        at_lane = lane == k
        pivot_row = jnp.where(at_lane[0:1], 1.0, matrix[k:k + 1, :]) * scale
        rest = jnp.where(at_lane, 0.0, matrix) - matrix[:, k:k + 1] * pivot_row
        matrix = jnp.where(sub == k, pivot_row, rest)
    inverse_ref[...] = matrix
    weights = jnp.sum(matrix * quad, axis=0, keepdims=True)
    weights_ref[...] = weights
    solved_rows = solved_rows_ref[...]
    shift_ref[...] = jnp.dot(
        jnp.broadcast_to(weights, (8, NEW)), solved_rows, precision=HIGH, preferred_element_type=jnp.float32
    )[0:1]
    left = jnp.dot(matrix, solved_rows, precision=HIGH, preferred_element_type=jnp.float32)
    update_ref[...] = lax.dot_general(
        left, solved_cols_ref[...], (((0,), (0,)), ((), ())), precision=HIGH, preferred_element_type=jnp.float32
    )


def on_device(inverse_kernel, points, candidates, obs_embed, cand_embed, chosen):
    rows, cols = inverse_kernel.shape
    f32 = jnp.float32
    vmem = pl.BlockSpec(memory_space=pltpu.VMEM)
    dma = pltpu.SemaphoreType.DMA
    chosen_col = chosen.reshape(NEW, 1)
    total, solved_cols, solved_rows = pl.pallas_call(
        exchange_kernel,
        out_shape=(
            jax.ShapeDtypeStruct((NEW, 128), f32),
            jax.ShapeDtypeStruct((NEW, cols), f32),
            jax.ShapeDtypeStruct((NEW, rows), f32),
        ),
        in_specs=[pl.BlockSpec(memory_space=pl.ANY), vmem, vmem, vmem, vmem],
        out_specs=(vmem, vmem, vmem),
        scratch_shapes=[
            pltpu.VMEM((rows, cols), f32),
            pltpu.VMEM((2, NEW, 128), f32),
            pltpu.VMEM((2, 8, 8, 128), f32),
            pltpu.VMEM((2, 8, 128), f32),
            pltpu.VMEM((2, NX, NC, 8, 8, 128), f32),
            pltpu.VMEM((NEW, 128), f32),
            pltpu.VMEM((8, 8, 128), f32),
            pltpu.VMEM((1, 128), f32),
            pltpu.VMEM((8, 1, 128), f32),
            pltpu.VMEM((8, 8, 128), f32),
            pltpu.VMEM((NEW, 128), f32),
            pltpu.VMEM((8, NEW, 128), f32),
            dma((2, 8)), dma((2, 8)),
            dma((2, NZ)), dma((2, NC, 8)),
            dma((2, NX)), dma((2, NX)),
            dma((8,)), dma((8,)),
            dma((8,)), dma((8,)),
            dma((8,)), dma((8,)),
            dma, dma,
            dma((NZ,)), dma((8,)),
            dma,
        ],
        compiler_params=pltpu.CompilerParams(collective_id=0, has_side_effects=True),
    )(inverse_kernel, points, candidates, obs_embed.reshape(1, rows), chosen_col)
    update, inverse, weights, shift = pl.pallas_call(
        finish_kernel,
        out_shape=(
            jax.ShapeDtypeStruct((rows, cols), f32),
            jax.ShapeDtypeStruct((NEW, NEW), f32),
            jax.ShapeDtypeStruct((1, NEW), f32),
            jax.ShapeDtypeStruct((1, rows), f32),
        ),
        in_specs=[vmem] * 5,
        out_specs=(vmem,) * 4,
    )(total, solved_cols, solved_rows, chosen_col, cand_embed.reshape(1, -1))
    return update, inverse, weights.reshape(NEW), shift.reshape(rows)


def solution(mesh):
    return jax.shard_map(
        on_device,
        mesh=mesh,
        in_specs=(P("row", "col"), P("row", "col"), P(None, "col"), P("row"), P(), P()),
        out_specs=(P("row", "col"), P(), P(), P("row")),
        check_vma=False,
    )
```

time: 505 us -> 69.1 us (0.14)
  the two profiles are of different devices: /device:TPU:8 before, /device:TPU:1 now
where the time goes in v1:
time: 69.1 us; the launch traced here: 69 us
  Pallas kernels  67 us (97%)
  local copies, waits for them, and re-layouts  1.36 us (2%)
    pallas_call x1, Pallas kernels, on_device(): pl.pallas_call(exchange_kernel, out_shape=(jax.ShapeDtypeStruct((NEW, 128...  59 us
    pallas_call x1, Pallas kernels, on_device(): pl.pallas_call(finish_kernel, out_shape=(jax.ShapeDtypeStruct((rows, cols...  8.01 us

profile of v1, /device:TPU:1, one launch (start us, length us, event | category | flops | bytes accessed | tf_op | source)
XLA Modules:
  0.0 69.0 jit_solution(14582017634974775073)
XLA Ops:
  0.6 0.0 copy-start
  0.6 0.6 copy-done
  1.3 0.7 %copy.10.chosen_ref = s32[64,1]{1,0:T(8,128)} copy(s32[64,1]{0,1:T(1,128)S(1)} %bitcast.6) | data formatting | bytes 512 | tf_op jit(solution)/shard_map/reshape | solution.py:282
  2.0 59.0 %shard_map.93 = (f32[64,128]{1,0:T(8,128)}, f32[64,1024]{1,0:T(8,128)}, f32[64,128]{1,0:T(8,128)}) custom-call(f32[128,1024]{1,0:T(8,128)} %inv_hbm.1, bf16[128,128]{1,0:T(8,128)(2,1)} %points_ref.1, bf16[1024,128]{1,0:T(8,128)(2,1)} %cand_ref.1, f32[1,128]{1,0:T(1,128)} %bitcast.7, s32[64,1]{1,0:T(8,128)} %copy.10.chosen_ref), custom_call_target="tpu_custom_call" | custom-call | tf_op jit(solution)/shard_map/pallas_call | solution.py:283
  61.0 8.0 %shard_map.94 = (f32[128,1024]{1,0:T(8,128)}, f32[64,64]{1,0:T(8,128)}, f32[1,64]{1,0:T(1,128)}, f32[1,128]{1,0:T(1,128)}) custom-call(f32[64,128]{1,0:T(8,128)} %get-tuple-element.11.total_ref, f32[64,1024]{1,0:T(8,128)} %get-tuple-element.12.solved_cols_ref, f32[64,128]{1,0:T(8,128)} %get-tuple-element.13.solved_rows_ref, s32[64,1]{1,0:T(8,128)} %copy.10.chosen_ref, ...), custom_call_target="tpu_custom_call" | custom-call | tf_op jit(solution)/shard_map/pallas_call | solution.py:317
Async XLA Ops:
  0.6 0.7 copy-start

commit v2 on v1

--- a/solution.py
+++ b/solution.py
@@ -10,6 +10,9 @@
 NX, NY, NZ, NC = 4, 4, 16, 2
 NOBS = 8192
 NEW = 64
+HALF = NEW // 2
+FAR = (8, 7, -7, 6, -6, 5, -5, 4, -4, 3, -3, 2, -2, 1, -1, 0)
+GROUP = 4
 
 
 def matern(square):
@@ -24,7 +27,7 @@
 
 
 def exchange_kernel(
-    inv_hbm, points_ref, cand_ref, embed_ref, chosen_ref,
+    inv_hbm, points_ref, cand_ref, embed_ref, chosen_ref, cand_embed_ref,
     total_ref, solved_cols_ref, solved_rows_ref,
     inv, a2a_src, a2a_rcv, tile, full, gsrc, grcv, etr, ebuf, srow, fsrc, frcv,
     ss_a, rs_a, ss_z, rs_z, ss_x, rs_x, ss_g, rs_g, ss_r, rs_r, ss_f, rs_f, ss_e, rs_e, ss_ez, rs_ez, inv_sem,
@@ -83,9 +86,11 @@
     for k in range(4):
         greet(k * NZ + z, col, x == k)
 
-    onehot = (chosen_ref[...] == lax.broadcasted_iota(jnp.int32, (NEW, cand_ref.shape[0]), 1))
-    onehot = jnp.where(onehot, 1.0, 0.0).astype(jnp.bfloat16)
-    appended = jnp.dot(onehot, cand_ref[...], preferred_element_type=jnp.float32).astype(jnp.bfloat16)
+    onehot = (chosen_ref[...] == lax.broadcasted_iota(jnp.int32, (cand_ref.shape[0], NEW), 0))
+    onehot = jnp.where(onehot, 1.0, 0.0)
+    appended = lax.dot_general(
+        onehot.astype(jnp.bfloat16), cand_ref[...], (((0,), (0,)), ((), ())), preferred_element_type=jnp.float32
+    ).astype(jnp.bfloat16)
     pts = points_ref[...]
     wide = pts.astype(jnp.float32)
     sq_obs = dot_t(jnp.ones((8, wide.shape[1]), jnp.float32), wide * wide, HIGH)[0:1]
@@ -97,6 +102,7 @@
     a2a_src[0] = sq_obs + sq_col - 2.0 * dot_t(appended, pts)
     gsrc[:, 0:NEW] = sq_row + sq_col - 2.0 * pair
     gsrc[:, NEW:] = jnp.zeros((NEW, NEW), jnp.float32)
+    fsrc[HALF:, NEW:] = jnp.zeros((8, NEW), jnp.float32)
 
     pl.semaphore_wait(barrier, 41 - 2 * on_diag.astype(jnp.int32) - home.astype(jnp.int32) + 1)
 
@@ -111,12 +117,15 @@
 
     def z_args(p, k):
         return (
-            tile.at[p], full.at[p, x, core, spot], ss_z.at[p, k], rs_z.at[p, core, spot],
-            x * NZ + k, y * NC + half, jnp.logical_and(home, z == k),
-        )
-
-    def x_args(p, k):
-        return (full.at[p, x], full.at[p, x], ss_x.at[p, k], rs_x.at[p, x], k * NZ + z, col)
+            tile.at[p], full.at[p, x, spot, core], ss_z.at[p, k], rs_z.at[p, spot, core],
+            x * NZ + (z + FAR[k]) % NZ, y * NC + half, jnp.logical_and(home, FAR[k] == 0),
+        )
+
+    def x_copy(p, k, s):
+        return pltpu.make_async_remote_copy(
+            src_ref=full.at[p, x, s], dst_ref=full.at[p, x, s], send_sem=ss_x.at[p, k, s], recv_sem=rs_x.at[p, x, s],
+            device_id=(((x + k) % NX) * NZ + z, col), device_id_type=MESH,
+        )
 
     def e_args():
         return (embed_ref, etr, ss_e, rs_e, y * NZ + z, x * NC + core, on_diag)
@@ -150,25 +159,23 @@
             send(*z_args(p, k))
 
     def spread_x(p):
-        for c in range(NC):
+        for d in reversed(FAR):
+            origin = (z + d) % NZ
+            s = origin % 8
+
+            @pl.when(origin // 8 == core)
+            def _():
+                for c in range(NC):
+                    arrived(full.at[p, x, s, c], rs_z.at[p, s, c])
+                for k in (2, 1, 3):
+                    x_copy(p, k, s).start()
+
+    def spread_done(p):
+        for k in (1, 3, 2):
+            other = (x + k) % NX
             for s in range(8):
-                arrived(full.at[p, x, c, s], rs_z.at[p, c, s])
-        for k in range(NX):
-            src, dst, ssem, rsem, to_row, to_col = x_args(p, k)
-
-            @pl.when(x != k)
-            def _():
-                pltpu.make_async_remote_copy(
-                    src_ref=src, dst_ref=dst, send_sem=ssem, recv_sem=rsem,
-                    device_id=(to_row, to_col), device_id_type=MESH,
-                ).start()
-
-    def spread_done(p):
-        for k in range(NX):
-            @pl.when(x != k)
-            def _():
-                arrived(full.at[p, k], rs_x.at[p, k])
-        parts = [full[p, :, :, s].reshape(NEW, 128) for s in range(8)]
+                arrived(full.at[p, other, s], rs_x.at[p, other, s])
+        parts = [full[p, :, s].reshape(NEW, 128) for s in range(8)]
         return jnp.concatenate(parts, axis=1)
 
     reduce_tiles(0)
@@ -192,6 +199,10 @@
     for k in range(1, 8):
         gram = gram + grcv[k]
     gram = matern(gram[:, 0:NEW]) * (1.0 / NEW)
+    gram = jnp.concatenate([gram, gram], axis=1)
+    gram = jnp.where(lax.broadcasted_iota(jnp.int32, (8, 128), 1) // NEW == col // 4, gram, 0.0)
+    cand_embed = jnp.broadcast_to(cand_embed_ref[...], (8, cand_ref.shape[0]))
+    new_embed = jnp.dot(cand_embed, onehot, precision=HIGH, preferred_element_type=jnp.float32)[0:1]
 
     spread_x(0)
     kernel_cols = spread_done(0)
@@ -207,10 +218,11 @@
     for s in range(8):
         arrived(ebuf.at[s], rs_ez.at[s])
     embed = jnp.concatenate([ebuf[s] for s in range(8)], axis=1)
-    fsrc[:, 0:NEW] = -dot_t(solved_cols, kernel_cols, HIGH)
-    fsrc[:, NEW:] = jnp.broadcast_to(jnp.sum(solved_cols * embed, axis=1, keepdims=True), (NEW, NEW))
-    slot = pl.ds(pl.multiple_of(8 * col, 8), 8)
-    fsrc[slot, 0:NEW] = fsrc[slot, 0:NEW] + gram
+    term = -dot_t(solved_cols, kernel_cols, HIGH)
+    fsrc[0:HALF] = jnp.concatenate([term[0:HALF], term[HALF:]], axis=1)
+    fsrc[HALF:HALF + 8, 0:NEW] = dot_t(jnp.broadcast_to(embed, (8, embed.shape[1])), solved_cols, HIGH)
+    slot = pl.ds(pl.multiple_of(8 * (col % 4), 8), 8)
+    fsrc[slot, :] = fsrc[slot, :] + gram
     for k in range(8):
         send(*f_args(k))
     solved_cols_ref[...] = solved_cols
@@ -222,7 +234,9 @@
     total = frcv[0]
     for k in range(1, 8):
         total = total + frcv[k]
-    total_ref[...] = total
+    total_ref[0:HALF] = total[0:HALF]
+    total_ref[HALF:, 0:NEW] = total[HALF:, 0:NEW] * (1.0 / NOBS) - new_embed
+    total_ref[HALF:, NEW:] = jnp.zeros((8, NEW), jnp.float32)
 
     wait_sent(*e_args())
     for p in range(2):
@@ -230,8 +244,9 @@
             wait_sent(*a2a_args(p, k))
         for k in range(NZ):
             wait_sent(*z_args(p, k))
-        for k in range(NX):
-            wait_sent(*x_args(p, k), x == k)
+        for k in (1, 2, 3):
+            for s in range(8):
+                x_copy(p, k, s).wait_send()
     for k in range(8):
         wait_sent(*g_args(k))
         wait_sent(*r_args(k))
@@ -244,23 +259,27 @@
 
 
 def finish_kernel(
-    total_ref, solved_cols_ref, solved_rows_ref, chosen_ref, cand_embed_ref,
-    update_ref, inverse_ref, weights_ref, shift_ref,
+    total_ref, solved_cols_ref, solved_rows_ref, update_ref, inverse_ref, weights_ref, shift_ref,
 ):
     total = total_ref[...]
     sub = lax.broadcasted_iota(jnp.int32, (NEW, NEW), 0)
     lane = lax.broadcasted_iota(jnp.int32, (NEW, NEW), 1)
-    matrix = total[:, 0:NEW] + jnp.where(sub == lane, 1.0, 0.0)
-    picked = chosen_ref[...] == lax.broadcasted_iota(jnp.int32, (NEW, cand_embed_ref.shape[1]), 1)
-    new_embed = jnp.sum(jnp.where(picked, cand_embed_ref[...], 0.0), axis=1, keepdims=True)
-    quad = total[:, NEW:NEW + 1] * (1.0 / NOBS) - new_embed
-    for k in range(NEW):
-        pivot = matrix[k:k + 1, k:k + 1]
-        scale = jnp.where(pivot > 0.0, 1.0 / pivot, jnp.nan)
-        at_lane = lane == k
-        pivot_row = jnp.where(at_lane[0:1], 1.0, matrix[k:k + 1, :]) * scale
-        rest = jnp.where(at_lane, 0.0, matrix) - matrix[:, k:k + 1] * pivot_row
-        matrix = jnp.where(sub == k, pivot_row, rest)
+    eye = sub == lane
+    matrix = jnp.concatenate([total[0:HALF, 0:NEW], total[0:HALF, NEW:]], axis=0) + jnp.where(eye, 1.0, 0.0)
+    quad = jnp.sum(jnp.where(eye, total[HALF:HALF + 1, 0:NEW], 0.0), axis=1, keepdims=True)
+    for base in range(0, NEW, GROUP):
+        columns = [jnp.broadcast_to(matrix[:, k:k + 1], (NEW, NEW)) for k in range(base, base + GROUP)]
+        for t in range(GROUP):
+            k = base + t
+            here = columns[t]
+            pivot = here[k:k + 1, :]
+            scale = jnp.where(pivot > 0.0, 1.0 / pivot, jnp.nan)
+            at_lane, at_sub = lane == k, sub == k
+            pivot_row = jnp.where(at_lane[0:1], 1.0, matrix[k:k + 1, :]) * scale
+            matrix = jnp.where(at_sub, pivot_row, jnp.where(at_lane, 0.0, matrix) - here * pivot_row)
+            for u in range(t + 1, GROUP):
+                factor = columns[u][k:k + 1, :] * scale
+                columns[u] = jnp.where(at_sub, factor, columns[u] - here * factor)
     inverse_ref[...] = matrix
     weights = jnp.sum(matrix * quad, axis=0, keepdims=True)
     weights_ref[...] = weights
@@ -279,32 +298,31 @@
     f32 = jnp.float32
     vmem = pl.BlockSpec(memory_space=pltpu.VMEM)
     dma = pltpu.SemaphoreType.DMA
-    chosen_col = chosen.reshape(NEW, 1)
     total, solved_cols, solved_rows = pl.pallas_call(
         exchange_kernel,
         out_shape=(
-            jax.ShapeDtypeStruct((NEW, 128), f32),
+            jax.ShapeDtypeStruct((HALF + 8, 128), f32),
             jax.ShapeDtypeStruct((NEW, cols), f32),
             jax.ShapeDtypeStruct((NEW, rows), f32),
         ),
-        in_specs=[pl.BlockSpec(memory_space=pl.ANY), vmem, vmem, vmem, vmem],
+        in_specs=[pl.BlockSpec(memory_space=pl.ANY)] + [vmem] * 5,
         out_specs=(vmem, vmem, vmem),
         scratch_shapes=[
             pltpu.VMEM((rows, cols), f32),
             pltpu.VMEM((2, NEW, 128), f32),
             pltpu.VMEM((2, 8, 8, 128), f32),
             pltpu.VMEM((2, 8, 128), f32),
-            pltpu.VMEM((2, NX, NC, 8, 8, 128), f32),
+            pltpu.VMEM((2, NX, 8, NC, 8, 128), f32),
             pltpu.VMEM((NEW, 128), f32),
             pltpu.VMEM((8, 8, 128), f32),
             pltpu.VMEM((1, 128), f32),
             pltpu.VMEM((8, 1, 128), f32),
             pltpu.VMEM((8, 8, 128), f32),
-            pltpu.VMEM((NEW, 128), f32),
-            pltpu.VMEM((8, NEW, 128), f32),
+            pltpu.VMEM((HALF + 8, 128), f32),
+            pltpu.VMEM((8, HALF + 8, 128), f32),
             dma((2, 8)), dma((2, 8)),
-            dma((2, NZ)), dma((2, NC, 8)),
-            dma((2, NX)), dma((2, NX)),
+            dma((2, NZ)), dma((2, 8, NC)),
+            dma((2, NX, 8)), dma((2, NX, 8)),
             dma((8,)), dma((8,)),
             dma((8,)), dma((8,)),
             dma((8,)), dma((8,)),
@@ -313,7 +331,8 @@
             dma,
         ],
         compiler_params=pltpu.CompilerParams(collective_id=0, has_side_effects=True),
-    )(inverse_kernel, points, candidates, obs_embed.reshape(1, rows), chosen_col)
+    )(inverse_kernel, points, candidates, obs_embed.reshape(1, rows),
+      chosen.reshape(1, NEW), cand_embed.reshape(1, -1))
     update, inverse, weights, shift = pl.pallas_call(
         finish_kernel,
         out_shape=(
@@ -322,9 +341,9 @@
             jax.ShapeDtypeStruct((1, NEW), f32),
             jax.ShapeDtypeStruct((1, rows), f32),
         ),
-        in_specs=[vmem] * 5,
+        in_specs=[vmem] * 3,
         out_specs=(vmem,) * 4,
-    )(total, solved_cols, solved_rows, chosen_col, cand_embed.reshape(1, -1))
+    )(total, solved_cols, solved_rows)
     return update, inverse, weights.reshape(NEW), shift.reshape(rows)
 
 

time: 69.1 us -> 62.1 us (0.90)
  Pallas kernels: 67 us -> 61.3 us
  local copies, waits for them, and re-layouts: 1.36 us -> 0 us
    pallas_call x1, Pallas kernels: 8.01 us -> 4.9 us  [on_device(): pl.pallas_call(finish_kernel, out_shape=(jax.ShapeDtypeStruct((rows, cols...]
    pallas_call x1, Pallas kernels: 59 us -> 56.4 us  [on_device(): pl.pallas_call(exchange_kernel, out_shape=(jax.ShapeDtypeStruct((HALF + 8...]
    reshape x1 -> x0, local copies, waits for them, and re-layouts: 0.71 us -> none  [on_device(): chosen_col = chosen.reshape(NEW, 1)]
where the time goes in v2:
time: 62.1 us; the launch traced here: 61.9 us
  Pallas kernels  61.3 us (99%)
  between operations  0.64 us (1%)
    pallas_call x1, Pallas kernels, on_device(): pl.pallas_call(exchange_kernel, out_shape=(jax.ShapeDtypeStruct((HALF + 8...  56.4 us
    pallas_call x1, Pallas kernels, on_device(): pl.pallas_call(finish_kernel, out_shape=(jax.ShapeDtypeStruct((rows, cols...  4.9 us

profile of v2, /device:TPU:1, one launch (start us, length us, event | category | flops | bytes accessed | tf_op | source)
XLA Modules:
  0.0 61.9 jit_solution(12113628945645107877)
XLA Ops:
  0.6 56.4 %shard_map.93 = (f32[40,128]{1,0:T(8,128)}, f32[64,1024]{1,0:T(8,128)}, f32[64,128]{1,0:T(8,128)}) custom-call(f32[128,1024]{1,0:T(8,128)} %inv_hbm.1, bf16[128,128]{1,0:T(8,128)(2,1)} %points_ref.1, bf16[1024,128]{1,0:T(8,128)(2,1)} %cand_ref.1, f32[1,128]{1,0:T(1,128)} %bitcast.6, s32[1,64]{1,0:T(1,128)} %bitcast.7, f32[1,1024]{1,0:T(1,128)} %bitcast.5), custom_call_target="tpu_custom_call" | custom-call | tf_op jit(solution)/shard_map/pallas_call | solution.py:301
  57.0 4.9 %shard_map.94 = (f32[128,1024]{1,0:T(8,128)}, f32[64,64]{1,0:T(8,128)}, f32[1,64]{1,0:T(1,128)}, f32[1,128]{1,0:T(1,128)}) custom-call(f32[40,128]{1,0:T(8,128)} %get-tuple-element.11.total_ref, f32[64,1024]{1,0:T(8,128)} %get-tuple-element.12.solved_cols_ref, f32[64,128]{1,0:T(8,128)} %get-tuple-element.13.solved_rows_ref), custom_call_target="tpu_custom_call" | custom-call | tf_op jit(solution)/shard_map/pallas_call | solution.py:336

commit v3 on v2

--- a/solution.py
+++ b/solution.py
@@ -10,7 +10,6 @@
 NX, NY, NZ, NC = 4, 4, 16, 2
 NOBS = 8192
 NEW = 64
-HALF = NEW // 2
 FAR = (8, 7, -7, 6, -6, 5, -5, 4, -4, 3, -3, 2, -2, 1, -1, 0)
 GROUP = 4
 
@@ -29,8 +28,8 @@
 def exchange_kernel(
     inv_hbm, points_ref, cand_ref, embed_ref, chosen_ref, cand_embed_ref,
     total_ref, solved_cols_ref, solved_rows_ref,
-    inv, a2a_src, a2a_rcv, tile, full, gsrc, grcv, etr, ebuf, srow, fsrc, frcv,
-    ss_a, rs_a, ss_z, rs_z, ss_x, rs_x, ss_g, rs_g, ss_r, rs_r, ss_f, rs_f, ss_e, rs_e, ss_ez, rs_ez, inv_sem,
+    inv, inv_hi, inv_lo, a2a_src, a2a_rcv, tile, full, gsrc, grcv, gram, etr, ebuf, srow, fsrc, frcv, tot,
+    ss_a, rs_a, ss_z, rs_z, ss_x, rs_x, ss_g, rs_g, ss_r, rs_r, ss_f, rs_f, ss_t, rs_t, ss_e, rs_e, ss_ez, rs_ez, inv_sem,
 ):
     row = lax.axis_index("row")
     col = lax.axis_index("col")
@@ -39,6 +38,8 @@
     half = z // 8
     spot = z % 8
     mine = 2 * x + core
+    quarter = (x + 2) % NX
+    own = (x, quarter)
     on_diag = x == y
     home = core == half
 
@@ -102,28 +103,34 @@
     a2a_src[0] = sq_obs + sq_col - 2.0 * dot_t(appended, pts)
     gsrc[:, 0:NEW] = sq_row + sq_col - 2.0 * pair
     gsrc[:, NEW:] = jnp.zeros((NEW, NEW), jnp.float32)
-    fsrc[HALF:, NEW:] = jnp.zeros((8, NEW), jnp.float32)
 
     pl.semaphore_wait(barrier, 41 - 2 * on_diag.astype(jnp.int32) - home.astype(jnp.int32) + 1)
 
-    def a2a_args(p, e):
+    never = x < 0
+
+    def a2a_args(p, k, h):
+        q = (x + k) % NX
+        src = a2a_src.at[p, pl.ds(pl.multiple_of(16 * q + 8 * h, 8), 8)]
+        is_self = jnp.logical_and(on_diag, core == h) if (k + 2 * p) % NX == 0 else never
         return (
-            a2a_src.at[p, pl.ds(8 * e, 8)], a2a_rcv.at[p, col], ss_a.at[p, e], rs_a.at[p, col],
-            (e // 2) * NZ + z, x * NC + e % 2, jnp.logical_and(on_diag, mine == e),
+            src, a2a_rcv.at[p, col], ss_a.at[p, k, h], rs_a.at[p, col],
+            ((x + k + 2 * p) % NX) * NZ + z, x * NC + h, is_self,
         )
 
     def g_args(k):
-        return (gsrc.at[pl.ds(8 * k, 8)], grcv.at[col], ss_g.at[k], rs_g.at[col], row, jnp.int32(k), col == k)
+        src = gsrc.at[pl.ds(pl.multiple_of(16 * quarter + 8 * k, 8), 8)]
+        return (src, grcv.at[col], ss_g.at[k], rs_g.at[col], row, jnp.int32(k), col == k)
 
     def z_args(p, k):
         return (
-            tile.at[p], full.at[p, x, spot, core], ss_z.at[p, k], rs_z.at[p, spot, core],
+            tile.at[p], full.at[p, own[p], spot, core], ss_z.at[p, k], rs_z.at[p, spot, core],
             x * NZ + (z + FAR[k]) % NZ, y * NC + half, jnp.logical_and(home, FAR[k] == 0),
         )
 
     def x_copy(p, k, s):
         return pltpu.make_async_remote_copy(
-            src_ref=full.at[p, x, s], dst_ref=full.at[p, x, s], send_sem=ss_x.at[p, k, s], recv_sem=rs_x.at[p, x, s],
+            src_ref=full.at[p, own[p], s], dst_ref=full.at[p, own[p], s],
+            send_sem=ss_x.at[p, k, s], recv_sem=rs_x.at[p, own[p], s],
             device_id=(((x + k) % NX) * NZ + z, col), device_id_type=MESH,
         )
 
@@ -135,16 +142,18 @@
 
     def r_args(k):
         return (
-            tile.at[1], srow.at[mine], ss_r.at[k], rs_r.at[mine],
+            tile.at[1], srow.at[2 * quarter + core], ss_r.at[k], rs_r.at[2 * quarter + core],
             y * NZ + z, jnp.int32(k), jnp.logical_and(on_diag, col == k),
         )
 
     def f_args(k):
-        return (fsrc, frcv.at[col], ss_f.at[k], rs_f.at[col], row, jnp.int32(k), col == k)
-
-    def reduce_tiles(p):
-        for e in range(8):
-            send(*a2a_args(p, e))
+        return (fsrc, frcv.at[col], ss_f.at[k], rs_f.at[col], row, (col + k) % 8, never if k else col >= 0)
+
+    def t_copy(k):
+        return pltpu.make_async_remote_copy(
+            src_ref=tot.at[quarter], dst_ref=tot.at[quarter], send_sem=ss_t.at[k], recv_sem=rs_t.at[quarter],
+            device_id=(((x + k) % NX) * NZ + z, col), device_id_type=MESH,
+        )
 
     def reduced(p):
         for k in range(8):
@@ -166,21 +175,26 @@
             @pl.when(origin // 8 == core)
             def _():
                 for c in range(NC):
-                    arrived(full.at[p, x, s, c], rs_z.at[p, s, c])
+                    arrived(full.at[p, own[p], s, c], rs_z.at[p, s, c])
                 for k in (2, 1, 3):
                     x_copy(p, k, s).start()
 
-    def spread_done(p):
-        for k in (1, 3, 2):
-            other = (x + k) % NX
-            for s in range(8):
-                arrived(full.at[p, other, s], rs_x.at[p, other, s])
-        parts = [full[p, :, s].reshape(NEW, 128) for s in range(8)]
-        return jnp.concatenate(parts, axis=1)
-
-    reduce_tiles(0)
+    def x_arrived(p, k):
+        other = (own[p] + k) % NX
+        for s in range(8):
+            arrived(full.at[p, other, s], rs_x.at[p, other, s])
+
+    def block(p, q):
+        return jnp.concatenate([full[p, q, s].reshape(16, 128) for s in range(8)], axis=1)
+
+    def columns(p):
+        return jnp.concatenate([full[p, :, s].reshape(NEW, 128) for s in range(8)], axis=1)
+
+    for k in (2, 1, 3, 0):
+        for h in range(NC):
+            send(*a2a_args(0, k, h))
     send(*e_args())
-    for k in range(8):
+    for k in range(2):
         send(*g_args(k))
 
     tile[0] = matern(reduced(0)) * (1.0 / (18.0 * NOBS))
@@ -193,39 +207,51 @@
         for k in range(NZ):
             send(*ez_args(k))
 
-    for k in range(8):
-        arrived(grcv.at[k], rs_g.at[k])
-    gram = grcv[0]
-    for k in range(1, 8):
-        gram = gram + grcv[k]
-    gram = matern(gram[:, 0:NEW]) * (1.0 / NEW)
-    gram = jnp.concatenate([gram, gram], axis=1)
-    gram = jnp.where(lax.broadcasted_iota(jnp.int32, (8, 128), 1) // NEW == col // 4, gram, 0.0)
+    gram[...] = jnp.zeros((16, 128), jnp.float32)
+
+    @pl.when(col < 2)
+    def _():
+        for k in range(8):
+            arrived(grcv.at[k], rs_g.at[k])
+        value = grcv[0]
+        for k in range(1, 8):
+            value = value + grcv[k]
+        gram[pl.ds(pl.multiple_of(8 * (col % 2), 8), 8), 0:NEW] = matern(value[:, 0:NEW]) * (1.0 / NEW)
+
     cand_embed = jnp.broadcast_to(cand_embed_ref[...], (8, cand_ref.shape[0]))
     new_embed = jnp.dot(cand_embed, onehot, precision=HIGH, preferred_element_type=jnp.float32)[0:1]
+    new_embed = jnp.sum(jnp.where(eye, new_embed, 0.0), axis=1, keepdims=True)
+    inv_copy.wait()
+    whole = inv[...]
+    inv_hi[...] = whole.astype(jnp.bfloat16)
+    inv_lo[...] = (whole - whole.astype(jnp.bfloat16).astype(jnp.float32)).astype(jnp.bfloat16)
 
     spread_x(0)
-    kernel_cols = spread_done(0)
-    inv_copy.wait()
-    a2a_src[1] = dot_t(kernel_cols, inv[...], HIGH)
-    reduce_tiles(1)
+    for k in (0, 1, 3, 2):
+        if k:
+            x_arrived(0, k)
+        q = (x + k) % NX
+        value = block(0, q)
+        hi = value.astype(jnp.bfloat16)
+        lo = (value - hi.astype(jnp.float32)).astype(jnp.bfloat16)
+        both = dot_t(jnp.concatenate([hi, lo], axis=0), inv_hi[...])
+        a2a_src[1, pl.ds(pl.multiple_of(16 * q, 8), 16)] = both[0:16] + both[16:32] + dot_t(hi, inv_lo[...])
+        for h in range(NC):
+            send(*a2a_args(1, k, h))
+    kernel_cols = columns(0)
+    for s in range(8):
+        arrived(ebuf.at[s], rs_ez.at[s])
+    embed = jnp.concatenate([ebuf[s] for s in range(8)], axis=1)
     tile[1] = reduced(1)
     spread_z(1)
     for k in range(8):
         send(*r_args(k))
     spread_x(1)
-    solved_cols = spread_done(1)
-    for s in range(8):
-        arrived(ebuf.at[s], rs_ez.at[s])
-    embed = jnp.concatenate([ebuf[s] for s in range(8)], axis=1)
-    term = -dot_t(solved_cols, kernel_cols, HIGH)
-    fsrc[0:HALF] = jnp.concatenate([term[0:HALF], term[HALF:]], axis=1)
-    fsrc[HALF:HALF + 8, 0:NEW] = dot_t(jnp.broadcast_to(embed, (8, embed.shape[1])), solved_cols, HIGH)
-    slot = pl.ds(pl.multiple_of(8 * (col % 4), 8), 8)
-    fsrc[slot, :] = fsrc[slot, :] + gram
-    for k in range(8):
+    solved = block(1, quarter)
+    fsrc[:, 0:NEW] = gram[:, 0:NEW] - dot_t(solved, kernel_cols, HIGH)
+    fsrc[:, NEW:] = jnp.broadcast_to(jnp.sum(solved * embed, axis=1, keepdims=True), (16, NEW))
+    for k in (4, 3, 5, 2, 6, 1, 7, 0):
         send(*f_args(k))
-    solved_cols_ref[...] = solved_cols
     for k in range(8):
         arrived(srow.at[k], rs_r.at[k])
     solved_rows_ref[...] = srow[...].reshape(NEW, 128)
@@ -234,21 +260,34 @@
     total = frcv[0]
     for k in range(1, 8):
         total = total + frcv[k]
-    total_ref[0:HALF] = total[0:HALF]
-    total_ref[HALF:, 0:NEW] = total[HALF:, 0:NEW] * (1.0 / NOBS) - new_embed
-    total_ref[HALF:, NEW:] = jnp.zeros((8, NEW), jnp.float32)
+    tot[quarter] = total
+    for k in (2, 1, 3):
+        t_copy(k).start()
+    for k in (1, 3, 2):
+        x_arrived(1, k)
+    solved_cols_ref[...] = columns(1)
+    for k in (1, 3, 2):
+        other = (quarter + k) % NX
+        arrived(tot.at[other], rs_t.at[other])
+    total = tot[...].reshape(NEW, 128)
+    total_ref[:, 0:NEW] = total[:, 0:NEW]
+    total_ref[:, NEW:] = total[:, NEW:] * (1.0 / NOBS) - new_embed
 
     wait_sent(*e_args())
     for p in range(2):
-        for k in range(8):
-            wait_sent(*a2a_args(p, k))
+        for k in range(NX):
+            for h in range(NC):
+                wait_sent(*a2a_args(p, k, h))
         for k in range(NZ):
             wait_sent(*z_args(p, k))
         for k in (1, 2, 3):
             for s in range(8):
                 x_copy(p, k, s).wait_send()
+    for k in (1, 2, 3):
+        t_copy(k).wait_send()
+    for k in range(2):
+        wait_sent(*g_args(k))
     for k in range(8):
-        wait_sent(*g_args(k))
         wait_sent(*r_args(k))
         wait_sent(*f_args(k))
 
@@ -265,8 +304,8 @@
     sub = lax.broadcasted_iota(jnp.int32, (NEW, NEW), 0)
     lane = lax.broadcasted_iota(jnp.int32, (NEW, NEW), 1)
     eye = sub == lane
-    matrix = jnp.concatenate([total[0:HALF, 0:NEW], total[0:HALF, NEW:]], axis=0) + jnp.where(eye, 1.0, 0.0)
-    quad = jnp.sum(jnp.where(eye, total[HALF:HALF + 1, 0:NEW], 0.0), axis=1, keepdims=True)
+    matrix = total[:, 0:NEW] + jnp.where(eye, 1.0, 0.0)
+    quad = total[:, NEW:NEW + 1]
     for base in range(0, NEW, GROUP):
         columns = [jnp.broadcast_to(matrix[:, k:k + 1], (NEW, NEW)) for k in range(base, base + GROUP)]
         for t in range(GROUP):
@@ -301,7 +340,7 @@
     total, solved_cols, solved_rows = pl.pallas_call(
         exchange_kernel,
         out_shape=(
-            jax.ShapeDtypeStruct((HALF + 8, 128), f32),
+            jax.ShapeDtypeStruct((NEW, 128), f32),
             jax.ShapeDtypeStruct((NEW, cols), f32),
             jax.ShapeDtypeStruct((NEW, rows), f32),
         ),
@@ -309,23 +348,28 @@
         out_specs=(vmem, vmem, vmem),
         scratch_shapes=[
             pltpu.VMEM((rows, cols), f32),
+            pltpu.VMEM((rows, cols), jnp.bfloat16),
+            pltpu.VMEM((rows, cols), jnp.bfloat16),
             pltpu.VMEM((2, NEW, 128), f32),
             pltpu.VMEM((2, 8, 8, 128), f32),
             pltpu.VMEM((2, 8, 128), f32),
             pltpu.VMEM((2, NX, 8, NC, 8, 128), f32),
             pltpu.VMEM((NEW, 128), f32),
             pltpu.VMEM((8, 8, 128), f32),
+            pltpu.VMEM((16, 128), f32),
             pltpu.VMEM((1, 128), f32),
             pltpu.VMEM((8, 1, 128), f32),
             pltpu.VMEM((8, 8, 128), f32),
-            pltpu.VMEM((HALF + 8, 128), f32),
-            pltpu.VMEM((8, HALF + 8, 128), f32),
-            dma((2, 8)), dma((2, 8)),
+            pltpu.VMEM((16, 128), f32),
+            pltpu.VMEM((8, 16, 128), f32),
+            pltpu.VMEM((NX, 16, 128), f32),
+            dma((2, NX, NC)), dma((2, 8)),
             dma((2, NZ)), dma((2, 8, NC)),
             dma((2, NX, 8)), dma((2, NX, 8)),
+            dma((2,)), dma((8,)),
             dma((8,)), dma((8,)),
             dma((8,)), dma((8,)),
-            dma((8,)), dma((8,)),
+            dma((NX,)), dma((NX,)),
             dma, dma,
             dma((NZ,)), dma((8,)),
             dma,

time: 62.1 us -> 59.5 us (0.958)
  Pallas kernels: 61.3 us -> 58.7 us
    pallas_call x1, Pallas kernels: 56.4 us -> 53.8 us  [on_device(): pl.pallas_call(exchange_kernel, out_shape=(jax.ShapeDtypeStruct((NEW, 128...]
where the time goes in v3:
time: 59.5 us; the launch traced here: 59.4 us
  Pallas kernels  58.7 us (99%)
  between operations  0.64 us (1%)
    pallas_call x1, Pallas kernels, on_device(): pl.pallas_call(exchange_kernel, out_shape=(jax.ShapeDtypeStruct((NEW, 128...  53.8 us
    pallas_call x1, Pallas kernels, on_device(): pl.pallas_call(finish_kernel, out_shape=(jax.ShapeDtypeStruct((rows, cols...  4.87 us

profile of v3, /device:TPU:1, one launch (start us, length us, event | category | flops | bytes accessed | tf_op | source)
XLA Modules:
  0.0 59.4 jit_solution(12346249345848181377)
XLA Ops:
  0.6 53.8 %shard_map.93 = (f32[64,128]{1,0:T(8,128)}, f32[64,1024]{1,0:T(8,128)}, f32[64,128]{1,0:T(8,128)}) custom-call(f32[128,1024]{1,0:T(8,128)} %inv_hbm.1, bf16[128,128]{1,0:T(8,128)(2,1)} %points_ref.1, bf16[1024,128]{1,0:T(8,128)(2,1)} %cand_ref.1, f32[1,128]{1,0:T(1,128)} %bitcast.6, s32[1,64]{1,0:T(1,128)} %bitcast.7, f32[1,1024]{1,0:T(1,128)} %bitcast.5), custom_call_target="tpu_custom_call" | custom-call | tf_op jit(solution)/shard_map/pallas_call | solution.py:340
  54.5 4.9 %shard_map.94 = (f32[128,1024]{1,0:T(8,128)}, f32[64,64]{1,0:T(8,128)}, f32[1,64]{1,0:T(1,128)}, f32[1,128]{1,0:T(1,128)}) custom-call(f32[64,128]{1,0:T(8,128)} %get-tuple-element.11.total_ref, f32[64,1024]{1,0:T(8,128)} %get-tuple-element.12.solved_cols_ref, f32[64,128]{1,0:T(8,128)} %get-tuple-element.13.solved_rows_ref), custom_call_target="tpu_custom_call" | custom-call | tf_op jit(solution)/shard_map/pallas_call | solution.py:380

commit v4 on v3

--- a/solution.py
+++ b/solution.py
@@ -29,7 +29,7 @@
     inv_hbm, points_ref, cand_ref, embed_ref, chosen_ref, cand_embed_ref,
     total_ref, solved_cols_ref, solved_rows_ref,
     inv, inv_hi, inv_lo, a2a_src, a2a_rcv, tile, full, gsrc, grcv, gram, etr, ebuf, srow, fsrc, frcv, tot,
-    ss_a, rs_a, ss_z, rs_z, ss_x, rs_x, ss_g, rs_g, ss_r, rs_r, ss_f, rs_f, ss_t, rs_t, ss_e, rs_e, ss_ez, rs_ez, inv_sem,
+    ss_a, rs_a, ss_z, rs_z, ss_x, rs_x, ss_g, rs_g, ss_r, rs_r, ss_f, rs_f, ss_t, rs_t, ss_e, rs_e, ss_ez, rs_ez, inv_sem, out_sem, scols, srows, ready,
 ):
     row = lax.axis_index("row")
     col = lax.axis_index("col")
@@ -82,8 +82,9 @@
         greet(y * NZ + z, jnp.int32(k), jnp.logical_and(on_diag, col == k))
         greet((k // 2) * NZ + z, x * NC + k % 2, jnp.logical_and(on_diag, mine == k))
         greet(row, jnp.int32(k), col == k)
-    for k in range(16):
-        greet(x * NZ + core * 8 + k // 2, y * NC + k % 2, jnp.logical_and(row % NZ == core * 8 + k // 2, core == k % 2))
+    for d in (4, -4, 3, -3, 2, -2, 1, -1):
+        for h in range(NC):
+            greet(x * NZ + (z + d) % NZ, y * NC + h, x < 0)
     for k in range(4):
         greet(k * NZ + z, col, x == k)
 
@@ -95,16 +96,14 @@
     pts = points_ref[...]
     wide = pts.astype(jnp.float32)
     sq_obs = dot_t(jnp.ones((8, wide.shape[1]), jnp.float32), wide * wide, HIGH)[0:1]
-    pair = dot_t(appended, appended)
     eye = lax.broadcasted_iota(jnp.int32, (NEW, NEW), 0) == lax.broadcasted_iota(jnp.int32, (NEW, NEW), 1)
-    diagonal = jnp.where(eye, pair, 0.0)
-    sq_col = jnp.sum(diagonal, axis=1, keepdims=True)
-    sq_row = jnp.sum(diagonal, axis=0, keepdims=True)
+    new = appended.astype(jnp.float32)
+    sq_col = jnp.sum(new * new, axis=1, keepdims=True)
     a2a_src[0] = sq_obs + sq_col - 2.0 * dot_t(appended, pts)
-    gsrc[:, 0:NEW] = sq_row + sq_col - 2.0 * pair
-    gsrc[:, NEW:] = jnp.zeros((NEW, NEW), jnp.float32)
-
-    pl.semaphore_wait(barrier, 41 - 2 * on_diag.astype(jnp.int32) - home.astype(jnp.int32) + 1)
+
+    pl.semaphore_wait(barrier, 42 - 2 * on_diag.astype(jnp.int32))
+    for d in (4, -4):
+        pl.semaphore_signal(ready, inc=1, device_id=(x * NZ + (z + d) % NZ, col), device_id_type=MESH)
 
     never = x < 0
 
@@ -194,11 +193,19 @@
         for h in range(NC):
             send(*a2a_args(0, k, h))
     send(*e_args())
+
+    pair = dot_t(appended, appended)
+    diagonal = jnp.where(eye, pair, 0.0)
+    sq_row = jnp.sum(diagonal, axis=0, keepdims=True)
+    sq_col = jnp.sum(diagonal, axis=1, keepdims=True)
+    gsrc[:, 0:NEW] = sq_row + sq_col - 2.0 * pair
+    gsrc[:, NEW:] = jnp.zeros((NEW, NEW), jnp.float32)
+
+    tile[0] = matern(reduced(0)) * (1.0 / (18.0 * NOBS))
+    pl.semaphore_wait(ready, 2)
+    spread_z(0)
     for k in range(2):
         send(*g_args(k))
-
-    tile[0] = matern(reduced(0)) * (1.0 / (18.0 * NOBS))
-    spread_z(0)
 
     arrived(etr, rs_e)
 
@@ -254,7 +261,9 @@
         send(*f_args(k))
     for k in range(8):
         arrived(srow.at[k], rs_r.at[k])
-    solved_rows_ref[...] = srow[...].reshape(NEW, 128)
+    srows[...] = srow[...].reshape(NEW, 128)
+    rows_out = pltpu.make_async_copy(srows, solved_rows_ref, out_sem.at[0])
+    rows_out.start()
     for k in range(8):
         arrived(frcv.at[k], rs_f.at[k])
     total = frcv[0]
@@ -265,7 +274,9 @@
         t_copy(k).start()
     for k in (1, 3, 2):
         x_arrived(1, k)
-    solved_cols_ref[...] = columns(1)
+    scols[...] = columns(1)
+    cols_out = pltpu.make_async_copy(scols, solved_cols_ref, out_sem.at[1])
+    cols_out.start()
     for k in (1, 3, 2):
         other = (quarter + k) % NX
         arrived(tot.at[other], rs_t.at[other])
@@ -273,6 +284,8 @@
     total_ref[:, 0:NEW] = total[:, 0:NEW]
     total_ref[:, NEW:] = total[:, NEW:] * (1.0 / NOBS) - new_embed
 
+    rows_out.wait()
+    cols_out.wait()
     wait_sent(*e_args())
     for p in range(2):
         for k in range(NX):
@@ -345,7 +358,7 @@
             jax.ShapeDtypeStruct((NEW, rows), f32),
         ),
         in_specs=[pl.BlockSpec(memory_space=pl.ANY)] + [vmem] * 5,
-        out_specs=(vmem, vmem, vmem),
+        out_specs=(vmem, pl.BlockSpec(memory_space=pl.ANY), pl.BlockSpec(memory_space=pl.ANY)),
         scratch_shapes=[
             pltpu.VMEM((rows, cols), f32),
             pltpu.VMEM((rows, cols), jnp.bfloat16),
@@ -373,6 +386,10 @@
             dma, dma,
             dma((NZ,)), dma((8,)),
             dma,
+            dma((2,)),
+            pltpu.VMEM((NEW, cols), f32),
+            pltpu.VMEM((NEW, rows), f32),
+            pltpu.SemaphoreType.REGULAR,
         ],
         compiler_params=pltpu.CompilerParams(collective_id=0, has_side_effects=True),
     )(inverse_kernel, points, candidates, obs_embed.reshape(1, rows),

time: 59.5 us -> 56.5 us (0.950)
  Pallas kernels: 58.7 us -> 55.7 us
    pallas_call x1, Pallas kernels: 53.8 us -> 50.8 us  [on_device(): pl.pallas_call(exchange_kernel, out_shape=(jax.ShapeDtypeStruct((NEW, 128...]
where the time goes in v4:
time: 56.5 us; the launch traced here: 56.3 us
  Pallas kernels  55.7 us (99%)
  between operations  0.64 us (1%)
    pallas_call x1, Pallas kernels, on_device(): pl.pallas_call(exchange_kernel, out_shape=(jax.ShapeDtypeStruct((NEW, 128...  50.8 us
    pallas_call x1, Pallas kernels, on_device(): pl.pallas_call(finish_kernel, out_shape=(jax.ShapeDtypeStruct((rows, cols...  4.87 us

profile of v4, /device:TPU:1, one launch (start us, length us, event | category | flops | bytes accessed | tf_op | source)
XLA Modules:
  0.0 56.3 jit_solution(15468807132237579130)
XLA Ops:
  0.6 50.8 %shard_map.93 = (f32[64,128]{1,0:T(8,128)}, f32[64,1024]{1,0:T(8,128)}, f32[64,128]{1,0:T(8,128)}) custom-call(f32[128,1024]{1,0:T(8,128)} %inv_hbm.1, bf16[128,128]{1,0:T(8,128)(2,1)} %points_ref.1, bf16[1024,128]{1,0:T(8,128)(2,1)} %cand_ref.1, f32[1,128]{1,0:T(1,128)} %bitcast.6, s32[1,64]{1,0:T(1,128)} %bitcast.7, f32[1,1024]{1,0:T(1,128)} %bitcast.5), custom_call_target="tpu_custom_call" | custom-call | tf_op jit(solution)/shard_map/pallas_call | solution.py:353
  51.5 4.9 %shard_map.94 = (f32[128,1024]{1,0:T(8,128)}, f32[64,64]{1,0:T(8,128)}, f32[1,64]{1,0:T(1,128)}, f32[1,128]{1,0:T(1,128)}) custom-call(f32[64,128]{1,0:T(8,128)} %get-tuple-element.11.total_ref, f32[64,1024]{1,0:T(8,128)} %get-tuple-element.12.solved_cols_ref, f32[64,128]{1,0:T(8,128)} %get-tuple-element.13.solved_rows_ref), custom_call_target="tpu_custom_call" | custom-call | tf_op jit(solution)/shard_map/pallas_call | solution.py:397

commit v5 on v4

--- a/solution.py
+++ b/solution.py
@@ -11,7 +11,7 @@
 NOBS = 8192
 NEW = 64
 FAR = (8, 7, -7, 6, -6, 5, -5, 4, -4, 3, -3, 2, -2, 1, -1, 0)
-GROUP = 4
+GROUP = 8
 
 
 def matern(square):
@@ -25,11 +25,17 @@
     )
 
 
+def split(value):
+    hi = value.astype(jnp.bfloat16)
+    return hi, (value - hi.astype(jnp.float32)).astype(jnp.bfloat16)
+
+
 def exchange_kernel(
-    inv_hbm, points_ref, cand_ref, embed_ref, chosen_ref, cand_embed_ref,
+    inv_hbm, points_hbm, cand_hbm, embed_hbm, chosen_hbm, cand_embed_hbm,
     total_ref, solved_cols_ref, solved_rows_ref,
     inv, inv_hi, inv_lo, a2a_src, a2a_rcv, tile, full, gsrc, grcv, gram, etr, ebuf, srow, fsrc, frcv, tot,
     ss_a, rs_a, ss_z, rs_z, ss_x, rs_x, ss_g, rs_g, ss_r, rs_r, ss_f, rs_f, ss_t, rs_t, ss_e, rs_e, ss_ez, rs_ez, inv_sem, out_sem, scols, srows, ready,
+    points_ref, cand_ref, embed_ref, chosen_ref, cand_embed_ref, in_sem,
 ):
     row = lax.axis_index("row")
     col = lax.axis_index("col")
@@ -68,6 +74,15 @@
     def arrived(dst, rsem):
         pltpu.make_async_copy(dst, dst, rsem).wait()
 
+    loads = [
+        pltpu.make_async_copy(src, dst, in_sem.at[k])
+        for k, (src, dst) in enumerate((
+            (chosen_hbm, chosen_ref), (cand_hbm, cand_ref), (points_hbm, points_ref),
+            (embed_hbm, embed_ref), (cand_embed_hbm, cand_embed_ref),
+        ))
+    ]
+    for load in loads:
+        load.start()
     inv_copy = pltpu.make_async_copy(inv_hbm, inv, inv_sem)
     inv_copy.start()
 
@@ -88,6 +103,8 @@
     for k in range(4):
         greet(k * NZ + z, col, x == k)
 
+    for load in loads:
+        load.wait()
     onehot = (chosen_ref[...] == lax.broadcasted_iota(jnp.int32, (cand_ref.shape[0], NEW), 0))
     onehot = jnp.where(onehot, 1.0, 0.0)
     appended = lax.dot_general(
@@ -95,7 +112,9 @@
     ).astype(jnp.bfloat16)
     pts = points_ref[...]
     wide = pts.astype(jnp.float32)
-    sq_obs = dot_t(jnp.ones((8, wide.shape[1]), jnp.float32), wide * wide, HIGH)[0:1]
+    ones = jnp.ones((8, wide.shape[1]), jnp.bfloat16)
+    sq_hi, sq_lo = split(wide * wide)
+    sq_obs = (dot_t(ones, sq_hi) + dot_t(ones, sq_lo))[0:1]
     eye = lax.broadcasted_iota(jnp.int32, (NEW, NEW), 0) == lax.broadcasted_iota(jnp.int32, (NEW, NEW), 1)
     new = appended.astype(jnp.float32)
     sq_col = jnp.sum(new * new, axis=1, keepdims=True)
@@ -229,9 +248,9 @@
     new_embed = jnp.dot(cand_embed, onehot, precision=HIGH, preferred_element_type=jnp.float32)[0:1]
     new_embed = jnp.sum(jnp.where(eye, new_embed, 0.0), axis=1, keepdims=True)
     inv_copy.wait()
-    whole = inv[...]
-    inv_hi[...] = whole.astype(jnp.bfloat16)
-    inv_lo[...] = (whole - whole.astype(jnp.bfloat16).astype(jnp.float32)).astype(jnp.bfloat16)
+    whole_hi, whole_lo = split(inv[...])
+    inv_hi[...] = whole_hi
+    inv_lo[...] = whole_lo
 
     spread_x(0)
     for k in (0, 1, 3, 2):
@@ -239,13 +258,12 @@
             x_arrived(0, k)
         q = (x + k) % NX
         value = block(0, q)
-        hi = value.astype(jnp.bfloat16)
-        lo = (value - hi.astype(jnp.float32)).astype(jnp.bfloat16)
+        hi, lo = split(value)
         both = dot_t(jnp.concatenate([hi, lo], axis=0), inv_hi[...])
         a2a_src[1, pl.ds(pl.multiple_of(16 * q, 8), 16)] = both[0:16] + both[16:32] + dot_t(hi, inv_lo[...])
         for h in range(NC):
             send(*a2a_args(1, k, h))
-    kernel_cols = columns(0)
+    kernel_hi, kernel_lo = split(columns(0))
     for s in range(8):
         arrived(ebuf.at[s], rs_ez.at[s])
     embed = jnp.concatenate([ebuf[s] for s in range(8)], axis=1)
@@ -255,7 +273,9 @@
         send(*r_args(k))
     spread_x(1)
     solved = block(1, quarter)
-    fsrc[:, 0:NEW] = gram[:, 0:NEW] - dot_t(solved, kernel_cols, HIGH)
+    hi, lo = split(solved)
+    both = dot_t(jnp.concatenate([hi, lo], axis=0), kernel_hi)
+    fsrc[:, 0:NEW] = gram[:, 0:NEW] - (both[0:16] + both[16:32] + dot_t(hi, kernel_lo))
     fsrc[:, NEW:] = jnp.broadcast_to(jnp.sum(solved * embed, axis=1, keepdims=True), (16, NEW))
     for k in (4, 3, 5, 2, 6, 1, 7, 0):
         send(*f_args(k))
@@ -311,8 +331,13 @@
 
 
 def finish_kernel(
-    total_ref, solved_cols_ref, solved_rows_ref, update_ref, inverse_ref, weights_ref, shift_ref,
+    total_ref, solved_cols_hbm, solved_rows_hbm, update_ref, inverse_ref, weights_ref, shift_ref,
+    solved_cols_ref, solved_rows_ref, sem,
 ):
+    cols_in = pltpu.make_async_copy(solved_cols_hbm, solved_cols_ref, sem.at[0])
+    rows_in = pltpu.make_async_copy(solved_rows_hbm, solved_rows_ref, sem.at[1])
+    rows_in.start()
+    cols_in.start()
     total = total_ref[...]
     sub = lax.broadcasted_iota(jnp.int32, (NEW, NEW), 0)
     lane = lax.broadcasted_iota(jnp.int32, (NEW, NEW), 1)
@@ -335,13 +360,19 @@
     inverse_ref[...] = matrix
     weights = jnp.sum(matrix * quad, axis=0, keepdims=True)
     weights_ref[...] = weights
+    rows_in.wait()
+    cols_in.wait()
     solved_rows = solved_rows_ref[...]
     shift_ref[...] = jnp.dot(
         jnp.broadcast_to(weights, (8, NEW)), solved_rows, precision=HIGH, preferred_element_type=jnp.float32
     )[0:1]
     left = jnp.dot(matrix, solved_rows, precision=HIGH, preferred_element_type=jnp.float32)
+    left_hi, left_lo = split(left)
+    cols_hi, cols_lo = split(solved_cols_ref[...])
     update_ref[...] = lax.dot_general(
-        left, solved_cols_ref[...], (((0,), (0,)), ((), ())), precision=HIGH, preferred_element_type=jnp.float32
+        jnp.concatenate([left_hi, left_hi, left_lo], axis=0),
+        jnp.concatenate([cols_hi, cols_lo, cols_hi], axis=0),
+        (((0,), (0,)), ((), ())), preferred_element_type=jnp.float32,
     )
 
 
@@ -357,7 +388,7 @@
             jax.ShapeDtypeStruct((NEW, cols), f32),
             jax.ShapeDtypeStruct((NEW, rows), f32),
         ),
-        in_specs=[pl.BlockSpec(memory_space=pl.ANY)] + [vmem] * 5,
+        in_specs=[pl.BlockSpec(memory_space=pl.ANY)] * 6,
         out_specs=(vmem, pl.BlockSpec(memory_space=pl.ANY), pl.BlockSpec(memory_space=pl.ANY)),
         scratch_shapes=[
             pltpu.VMEM((rows, cols), f32),
@@ -390,6 +421,12 @@
             pltpu.VMEM((NEW, cols), f32),
             pltpu.VMEM((NEW, rows), f32),
             pltpu.SemaphoreType.REGULAR,
+            pltpu.VMEM(points.shape, points.dtype),
+            pltpu.VMEM(candidates.shape, candidates.dtype),
+            pltpu.VMEM((1, rows), f32),
+            pltpu.VMEM((1, NEW), jnp.int32),
+            pltpu.VMEM((1, cand_embed.shape[0]), f32),
+            dma((5,)),
         ],
         compiler_params=pltpu.CompilerParams(collective_id=0, has_side_effects=True),
     )(inverse_kernel, points, candidates, obs_embed.reshape(1, rows),
@@ -402,8 +439,9 @@
             jax.ShapeDtypeStruct((1, NEW), f32),
             jax.ShapeDtypeStruct((1, rows), f32),
         ),
-        in_specs=[vmem] * 3,
+        in_specs=[vmem] + [pl.BlockSpec(memory_space=pl.ANY)] * 2,
         out_specs=(vmem,) * 4,
+        scratch_shapes=[pltpu.VMEM((NEW, cols), f32), pltpu.VMEM((NEW, rows), f32), dma((2,))],
     )(total, solved_cols, solved_rows)
     return update, inverse, weights.reshape(NEW), shift.reshape(rows)
 

time: 56.5 us -> 54.5 us (0.965)
  Pallas kernels: 55.7 us -> 53.6 us
    pallas_call x1, Pallas kernels: 4.87 us -> 3.55 us  [on_device(): pl.pallas_call(finish_kernel, out_shape=(jax.ShapeDtypeStruct((rows, cols...]
    pallas_call x1, Pallas kernels: 50.8 us -> 50.1 us  [on_device(): pl.pallas_call(exchange_kernel, out_shape=(jax.ShapeDtypeStruct((NEW, 128...]
where the time goes in v5:
time: 54.5 us; the launch traced here: 54.3 us
  Pallas kernels  53.6 us (98%)
  between operations  0.64 us (1%)
    pallas_call x1, Pallas kernels, on_device(): pl.pallas_call(exchange_kernel, out_shape=(jax.ShapeDtypeStruct((NEW, 128...  50.1 us
    pallas_call x1, Pallas kernels, on_device(): pl.pallas_call(finish_kernel, out_shape=(jax.ShapeDtypeStruct((rows, cols...  3.55 us

profile of v5, /device:TPU:1, one launch (start us, length us, event | category | flops | bytes accessed | tf_op | source)
XLA Modules:
  0.0 54.3 jit_solution(7453016068241272749)
XLA Ops:
  0.6 50.1 %shard_map.93 = (f32[64,128]{1,0:T(8,128)}, f32[64,1024]{1,0:T(8,128)}, f32[64,128]{1,0:T(8,128)}) custom-call(f32[128,1024]{1,0:T(8,128)} %inv_hbm.1, bf16[128,128]{1,0:T(8,128)(2,1)} %points_hbm.1, bf16[1024,128]{1,0:T(8,128)(2,1)} %cand_hbm.1, f32[1,128]{1,0:T(1,128)} %bitcast.6, s32[1,64]{1,0:T(1,128)} %bitcast.7, f32[1,1024]{1,0:T(1,128)} %bitcast.5), custom_call_target="tpu_custom_call" | custom-call | tf_op jit(solution)/shard_map/pallas_call | solution.py:384
  50.7 3.5 %shard_map.94 = (f32[128,1024]{1,0:T(8,128)}, f32[64,64]{1,0:T(8,128)}, f32[1,64]{1,0:T(1,128)}, f32[1,128]{1,0:T(1,128)}) custom-call(f32[64,128]{1,0:T(8,128)} %get-tuple-element.11.total_ref, f32[64,1024]{1,0:T(8,128)} %get-tuple-element.12.solved_cols_hbm, f32[64,128]{1,0:T(8,128)} %get-tuple-element.13.solved_rows_hbm), custom_call_target="tpu_custom_call" | custom-call | tf_op jit(solution)/shard_map/pallas_call | solution.py:434

commit v6 on v5

--- a/solution.py
+++ b/solution.py
@@ -93,29 +93,29 @@
         def _():
             pl.semaphore_signal(barrier, inc=1, device_id=(to_row, to_col), device_id_type=MESH)
 
+    for d in (4, -4, 3, -3, 2, -2, 1, -1):
+        for h in range(NC):
+            greet(x * NZ + (z + d) % NZ, y * NC + h, x < 0)
     for k in range(8):
         greet(y * NZ + z, jnp.int32(k), jnp.logical_and(on_diag, col == k))
         greet((k // 2) * NZ + z, x * NC + k % 2, jnp.logical_and(on_diag, mine == k))
         greet(row, jnp.int32(k), col == k)
-    for d in (4, -4, 3, -3, 2, -2, 1, -1):
-        for h in range(NC):
-            greet(x * NZ + (z + d) % NZ, y * NC + h, x < 0)
     for k in range(4):
         greet(k * NZ + z, col, x == k)
 
     for load in loads:
         load.wait()
-    onehot = (chosen_ref[...] == lax.broadcasted_iota(jnp.int32, (cand_ref.shape[0], NEW), 0))
-    onehot = jnp.where(onehot, 1.0, 0.0)
-    appended = lax.dot_general(
-        onehot.astype(jnp.bfloat16), cand_ref[...], (((0,), (0,)), ((), ())), preferred_element_type=jnp.float32
+    eye = lax.broadcasted_iota(jnp.int32, (NEW, NEW), 0) == lax.broadcasted_iota(jnp.int32, (NEW, NEW), 1)
+    index = jnp.sum(jnp.where(eye, chosen_ref[...].astype(jnp.float32), 0.0), axis=1, keepdims=True)
+    picked = index == lax.broadcasted_iota(jnp.int32, (NEW, cand_ref.shape[0]), 1).astype(jnp.float32)
+    appended = jnp.dot(
+        jnp.where(picked, 1.0, 0.0).astype(jnp.bfloat16), cand_ref[...], preferred_element_type=jnp.float32
     ).astype(jnp.bfloat16)
     pts = points_ref[...]
     wide = pts.astype(jnp.float32)
     ones = jnp.ones((8, wide.shape[1]), jnp.bfloat16)
     sq_hi, sq_lo = split(wide * wide)
     sq_obs = (dot_t(ones, sq_hi) + dot_t(ones, sq_lo))[0:1]
-    eye = lax.broadcasted_iota(jnp.int32, (NEW, NEW), 0) == lax.broadcasted_iota(jnp.int32, (NEW, NEW), 1)
     new = appended.astype(jnp.float32)
     sq_col = jnp.sum(new * new, axis=1, keepdims=True)
     a2a_src[0] = sq_obs + sq_col - 2.0 * dot_t(appended, pts)
@@ -244,9 +244,7 @@
             value = value + grcv[k]
         gram[pl.ds(pl.multiple_of(8 * (col % 2), 8), 8), 0:NEW] = matern(value[:, 0:NEW]) * (1.0 / NEW)
 
-    cand_embed = jnp.broadcast_to(cand_embed_ref[...], (8, cand_ref.shape[0]))
-    new_embed = jnp.dot(cand_embed, onehot, precision=HIGH, preferred_element_type=jnp.float32)[0:1]
-    new_embed = jnp.sum(jnp.where(eye, new_embed, 0.0), axis=1, keepdims=True)
+    new_embed = jnp.sum(jnp.where(picked, cand_embed_ref[...], 0.0), axis=1, keepdims=True)
     inv_copy.wait()
     whole_hi, whole_lo = split(inv[...])
     inv_hi[...] = whole_hi

time: 54.5 us -> 54.1 us (level)
  no operation moved by 1% of the time
where the time goes in v6:
time: 54.1 us; the launch traced here: 53.9 us
  Pallas kernels  53.3 us (99%)
  between operations  0.64 us (1%)
    pallas_call x1, Pallas kernels, on_device(): pl.pallas_call(exchange_kernel, out_shape=(jax.ShapeDtypeStruct((NEW, 128...  49.8 us
    pallas_call x1, Pallas kernels, on_device(): pl.pallas_call(finish_kernel, out_shape=(jax.ShapeDtypeStruct((rows, cols...  3.55 us

profile of v6, /device:TPU:1, one launch (start us, length us, event | category | flops | bytes accessed | tf_op | source)
XLA Modules:
  0.0 53.9 jit_solution(9862944586588580567)
XLA Ops:
  0.6 49.8 %shard_map.93 = (f32[64,128]{1,0:T(8,128)}, f32[64,1024]{1,0:T(8,128)}, f32[64,128]{1,0:T(8,128)}) custom-call(f32[128,1024]{1,0:T(8,128)} %inv_hbm.1, bf16[128,128]{1,0:T(8,128)(2,1)} %points_hbm.1, bf16[1024,128]{1,0:T(8,128)(2,1)} %cand_hbm.1, f32[1,128]{1,0:T(1,128)} %bitcast.6, s32[1,64]{1,0:T(1,128)} %bitcast.7, f32[1,1024]{1,0:T(1,128)} %bitcast.5), custom_call_target="tpu_custom_call" | custom-call | tf_op jit(solution)/shard_map/pallas_call | solution.py:382
  50.4 3.6 %shard_map.94 = (f32[128,1024]{1,0:T(8,128)}, f32[64,64]{1,0:T(8,128)}, f32[1,64]{1,0:T(1,128)}, f32[1,128]{1,0:T(1,128)}) custom-call(f32[64,128]{1,0:T(8,128)} %get-tuple-element.11.total_ref, f32[64,1024]{1,0:T(8,128)} %get-tuple-element.12.solved_cols_hbm, f32[64,128]{1,0:T(8,128)} %get-tuple-element.13.solved_rows_hbm), custom_call_target="tpu_custom_call" | custom-call | tf_op jit(solution)/shard_map/pallas_call | solution.py:432

commit v7 on v6

--- a/solution.py
+++ b/solution.py
@@ -329,8 +329,8 @@
 
 
 def finish_kernel(
-    total_ref, solved_cols_hbm, solved_rows_hbm, update_ref, inverse_ref, weights_ref, shift_ref,
-    solved_cols_ref, solved_rows_ref, sem,
+    total_ref, solved_cols_hbm, solved_rows_hbm, update_hbm, inverse_ref, weights_ref, shift_ref,
+    solved_cols_ref, solved_rows_ref, update_ref, sem,
 ):
     cols_in = pltpu.make_async_copy(solved_cols_hbm, solved_cols_ref, sem.at[0])
     rows_in = pltpu.make_async_copy(solved_rows_hbm, solved_rows_ref, sem.at[1])
@@ -367,11 +367,18 @@
     left = jnp.dot(matrix, solved_rows, precision=HIGH, preferred_element_type=jnp.float32)
     left_hi, left_lo = split(left)
     cols_hi, cols_lo = split(solved_cols_ref[...])
-    update_ref[...] = lax.dot_general(
-        jnp.concatenate([left_hi, left_hi, left_lo], axis=0),
-        jnp.concatenate([cols_hi, cols_lo, cols_hi], axis=0),
-        (((0,), (0,)), ((), ())), preferred_element_type=jnp.float32,
-    )
+    a = jnp.concatenate([left_hi, left_hi, left_lo], axis=0)
+    b = jnp.concatenate([cols_hi, cols_lo, cols_hi], axis=0)
+    copies = []
+    for k in range(2):
+        rows = pl.ds(64 * k, 64)
+        update_ref[rows, :] = lax.dot_general(
+            a[:, 64 * k:64 * k + 64], b, (((0,), (0,)), ((), ())), preferred_element_type=jnp.float32
+        )
+        copies.append(pltpu.make_async_copy(update_ref.at[rows], update_hbm.at[rows], sem.at[2 + k]))
+        copies[k].start()
+    for copy in copies:
+        copy.wait()
 
 
 def on_device(inverse_kernel, points, candidates, obs_embed, cand_embed, chosen):
@@ -438,8 +445,8 @@
             jax.ShapeDtypeStruct((1, rows), f32),
         ),
         in_specs=[vmem] + [pl.BlockSpec(memory_space=pl.ANY)] * 2,
-        out_specs=(vmem,) * 4,
-        scratch_shapes=[pltpu.VMEM((NEW, cols), f32), pltpu.VMEM((NEW, rows), f32), dma((2,))],
+        out_specs=(pl.BlockSpec(memory_space=pl.ANY), vmem, vmem, vmem),
+        scratch_shapes=[pltpu.VMEM((NEW, cols), f32), pltpu.VMEM((NEW, rows), f32), pltpu.VMEM((rows, cols), f32), dma((4,))],
     )(total, solved_cols, solved_rows)
     return update, inverse, weights.reshape(NEW), shift.reshape(rows)
 

time: 54.1 us -> 54.8 us (1.013)
  Pallas kernels: 53.3 us -> 53.9 us
    pallas_call x1, Pallas kernels: 3.55 us -> 4.16 us  [on_device(): pl.pallas_call(finish_kernel, out_shape=(jax.ShapeDtypeStruct((rows, cols...]
where the time goes in v7:
time: 54.8 us; the launch traced here: 54.6 us
  Pallas kernels  53.9 us (98%)
  between operations  0.64 us (1%)
    pallas_call x1, Pallas kernels, on_device(): pl.pallas_call(exchange_kernel, out_shape=(jax.ShapeDtypeStruct((NEW, 128...  49.8 us
    pallas_call x1, Pallas kernels, on_device(): pl.pallas_call(finish_kernel, out_shape=(jax.ShapeDtypeStruct((rows, cols...  4.16 us

profile of v7, /device:TPU:1, one launch (start us, length us, event | category | flops | bytes accessed | tf_op | source)
XLA Modules:
  0.0 54.6 jit_solution(13577848643638757313)
XLA Ops:
  0.6 49.8 %shard_map.93 = (f32[64,128]{1,0:T(8,128)}, f32[64,1024]{1,0:T(8,128)}, f32[64,128]{1,0:T(8,128)}) custom-call(f32[128,1024]{1,0:T(8,128)} %inv_hbm.1, bf16[128,128]{1,0:T(8,128)(2,1)} %points_hbm.1, bf16[1024,128]{1,0:T(8,128)(2,1)} %cand_hbm.1, f32[1,128]{1,0:T(1,128)} %bitcast.6, s32[1,64]{1,0:T(1,128)} %bitcast.7, f32[1,1024]{1,0:T(1,128)} %bitcast.5), custom_call_target="tpu_custom_call" | custom-call | tf_op jit(solution)/shard_map/pallas_call | solution.py:389
  50.4 4.2 %shard_map.94 = (f32[128,1024]{1,0:T(8,128)}, f32[64,64]{1,0:T(8,128)}, f32[1,64]{1,0:T(1,128)}, f32[1,128]{1,0:T(1,128)}) custom-call(f32[64,128]{1,0:T(8,128)} %get-tuple-element.11.total_ref, f32[64,1024]{1,0:T(8,128)} %get-tuple-element.12.solved_cols_hbm, f32[64,128]{1,0:T(8,128)} %get-tuple-element.13.solved_rows_hbm), custom_call_target="tpu_custom_call" | custom-call | tf_op jit(solution)/shard_map/pallas_call | solution.py:439
